TPU v7x, 256 devices: a whole 4x4x8 slice. The times are simulated.
256 devices in a mesh: group: 32 (over x, y, core), tp: 8 (over z).
Axes of the slice: x: 4, y: 4, z: 8, core: 2. Of those that a mesh axis runs over, the one named last changes fastest.
Arguments:
- hidden_in: bfloat16 [64, 3072], P('group'), may hold values from -6 to 6
- w_qkv: bfloat16 [3072, 2048], P(None, 'tp'), may hold values from -0.109375 to 0.109375
- w_out: bfloat16 [1536, 3072], P('tp'), may hold values from -0.15625 to 0.15625
- kv_pool: bfloat16 [2048, 128, 512], P(('group', 'tp'))
- page_table: int32 [64, 32], replicated, may hold values from 0 to 2047, as said below
- lengths: int32 [64], replicated, may hold values from 1 to 4096, as said below
Outputs:
- attn_proj: bfloat16 [64, 3072], P('group', 'tp')
Inputs may be any that keep to these rules, and one draw needn't show every extreme that they name: `page_table`: every pool slot is named by exactly one request page. `lengths`: some request has the full 32 * 128 cached tokens.
All inputs are finite; a program needn't handle non-finite values.
Results may differ from a plain program's by a relative error of at most 0.0085.
The roundings to bfloat16 on the way count: a program that leaves them out, or rounds other values in their place, can miss the bound.
Values may be sent and summed in bfloat16 or wider, within the bound.
A program may use at most 64 MiB of HBM per device.

v0:
```python
import jax
import jax.numpy as jnp
from jax import lax
from jax.sharding import PartitionSpec as P

HEADS = 12
KV_HEADS = 2
HEAD_DIM = 128


def on_device(hidden_in, w_qkv, w_out, kv_pool, page_table, lengths):
    qdim = HEADS * HEAD_DIM
    kdim = KV_HEADS * HEAD_DIM
    per_kv = HEADS // KV_HEADS
    scale = HEAD_DIM ** (-0.5)
    req_grp = hidden_in.shape[0]
    col_count = w_out.shape[0]
    col_start = lax.axis_index("tp") * col_count
    columns = jnp.dot(hidden_in, w_qkv, preferred_element_type=jnp.float32).astype(jnp.bfloat16)
    qkv = lax.all_gather(columns, "tp", axis=1, tiled=True)
    queries = lax.all_gather(qkv[:, :qdim], "group", axis=0, tiled=True)
    requests = queries.shape[0]
    slot_count = kv_pool.shape[0]
    page_len = kv_pool.shape[1]
    max_pages = page_table.shape[1]
    slot_ids = lax.axis_index(("group", "tp")) * slot_count + jnp.arange(
        slot_count, dtype=jnp.int32
    )
    match = page_table[:, :, None] == slot_ids[None, None, :]
    slot_req = jnp.sum(
        jnp.where(match, jnp.arange(requests, dtype=jnp.int32)[:, None, None], 0), axis=(0, 1)
    )
    slot_page = jnp.sum(
        jnp.where(match, jnp.arange(max_pages, dtype=jnp.int32)[None, :, None], 0), axis=(0, 1)
    )
    chosen = queries[slot_req].reshape(slot_count, KV_HEADS, per_kv, HEAD_DIM)
    keys = kv_pool[..., :kdim].reshape(slot_count, page_len, KV_HEADS, HEAD_DIM)
    values = kv_pool[..., kdim:].reshape(slot_count, page_len, KV_HEADS, HEAD_DIM)
    scores = jnp.einsum("pgjd,ptgd->pgjt", chosen, keys, preferred_element_type=jnp.float32) * scale
    position = slot_page[:, None] * page_len + jnp.arange(page_len, dtype=jnp.int32)[None, :]
    live = (position < lengths[slot_req][:, None])[:, None, None, :]
    top = jnp.max(jnp.where(live, scores, -1e30), axis=-1)
    probs = jnp.where(live, jnp.exp(scores - top[..., None]), 0.0).astype(jnp.bfloat16)
    total = jnp.sum(probs.astype(jnp.float32), axis=-1)
    weighted = jnp.einsum("pgjt,ptgd->pgjd", probs, values, preferred_element_type=jnp.float32)
    owner = slot_req[None, :] == jnp.arange(requests, dtype=jnp.int32)[:, None]
    req_top = jnp.max(jnp.where(owner[:, :, None, None], top[None], -1e30), axis=1)
    factor = jnp.exp(top - req_top[slot_req])
    onehot = owner.astype(jnp.float32)
    req_total = jnp.einsum(
        "rp,pgj->rgj", onehot, total * factor, precision=lax.Precision.HIGHEST
    ).reshape(requests, HEADS)
    req_sums = jnp.einsum(
        "rp,pgjd->rgjd", onehot, weighted * factor[..., None], precision=lax.Precision.HIGHEST
    ).reshape(requests, qdim)
    req_top = req_top.reshape(requests, HEADS)
    start = lax.axis_index("group") * req_grp
    peak_all = lax.pmax(req_top, ("group", "tp"))
    rescale = jnp.exp(req_top - peak_all)
    total_all, sums_all = lax.psum(
        (req_total * rescale, req_sums * jnp.repeat(rescale, HEAD_DIM, axis=1)), ("group", "tp")
    )
    peak = lax.dynamic_slice_in_dim(peak_all, start, req_grp, 0)
    whole = lax.dynamic_slice_in_dim(total_all, start, req_grp, 0)
    sums = lax.dynamic_slice_in_dim(sums_all, start, req_grp, 0)
    sums_part = lax.dynamic_slice_in_dim(sums, col_start, col_count, 1)
    own_q = qkv[:, :qdim].reshape(req_grp, KV_HEADS, per_kv, HEAD_DIM)
    own_k = qkv[:, qdim : qdim + kdim].reshape(req_grp, KV_HEADS, HEAD_DIM)
    own_v = qkv[:, qdim + kdim :].reshape(req_grp, KV_HEADS, HEAD_DIM)
    own_score = (
        jnp.einsum("rgjd,rgd->rgj", own_q, own_k, preferred_element_type=jnp.float32) * scale
    ).reshape(req_grp, HEADS)
    own_sums = jnp.broadcast_to(
        own_v.astype(jnp.float32)[:, :, None, :], (req_grp, KV_HEADS, per_kv, HEAD_DIM)
    ).reshape(req_grp, qdim)
    new_peak = jnp.maximum(peak, own_score)
    old_factor = jnp.exp(peak - new_peak)
    own_factor = jnp.exp(own_score - new_peak)
    new_whole = whole * old_factor + own_factor

    def pick(values_full):
        return lax.dynamic_slice_in_dim(values_full, col_start, col_count, 1)

    new_sums = sums_part * pick(jnp.repeat(old_factor, HEAD_DIM, axis=1)) + pick(
        own_sums * jnp.repeat(own_factor, HEAD_DIM, axis=1)
    )
    attn_part = (new_sums / pick(jnp.repeat(new_whole, HEAD_DIM, axis=1))).astype(jnp.bfloat16)
    partial_value = jnp.dot(attn_part, w_out, preferred_element_type=jnp.float32)
    return lax.psum_scatter(partial_value, "tp", scatter_dimension=1, tiled=True).astype(
        jnp.bfloat16
    )


def solution(mesh):
    in_specs = (
        P("group", None),
        P(None, "tp"),
        P("tp", None),
        P(("group", "tp"), None, None),
        P(),
        P(),
    )
    out_specs = P("group", "tp")
    return jax.shard_map(
        on_device, mesh=mesh, in_specs=in_specs, out_specs=out_specs, check_vma=False
    )
```

profile of v0, /device:TPU:2, one launch (start us, length us, event | category | flops | bytes accessed | tf_op | source)
XLA Modules:
  0.0 429.0 jit_solution(9588263399593622062)
XLA Ops:
  6.5 1.1 fusion.1
  7.7 0.2 copy-done
  8.0 1.0 convolution_convert_fusion
  9.0 19.1 %all_gather.6 = bf16[2,2048]{1,0:T(2,128)(2,1)S(1)} all-gather(bf16[2,256]{1,0:T(2,128)(2,1)S(1)} %convolution_convert_fusion), channel_id=1, replica_groups=mesh['group'=32,'tp'=8] {'tp'}, dimensions={1}, use_global_device_ids=true | all-gather | bytes 9216 | tf_op jit(solution)/shard_map/all_gather | solution.py:20
  28.1 24.7 %all-gather = bf16[32,2,1536]{2,1,0:T(2,128)(2,1)S(1)} all-gather(bf16[1,2,1536]{2,1,0:T(2,128)(2,1)S(1)} %get-tuple-element.19), channel_id=1, replica_groups=mesh['group'=32,'tp'=8] {'group'}, dimensions={0}, use_global_device_ids=true | all-gather | bytes 202752 | tf_op jit(solution)/shard_map/all_gather | solution.py:21
  52.9 0.6 gather_fusion
  53.5 0.6 gather_fusion.1
  54.1 1.3 fusion.25
  55.4 0.3 copy.96
  55.8 0.3 select_reduce_fusion
  56.1 0.1 copy.81
  56.2 0.1 select_reduce_fusion.1
  56.3 0.1 copy.82
  56.4 0.3 copy.97
  56.7 0.2 convert_reduce_fusion
  56.9 0.1 copy.86
  57.0 74.0 %pmax.7 = f32[64,12]{1,0:T(8,128)S(1)} all-reduce(f32[64,12]{1,0:T(8,128)S(1)} %copy.86), channel_id=1, replica_groups=mesh['group'=32,'tp'=8] {'group','tp'}, use_global_device_ids=true, to_apply=%region_4.5 | all-reduce | flops 768 | bytes 6144 | tf_op jit(solution)/shard_map/pmax | solution.py:58
  131.0 0.6 gather_fusion.2
  131.6 0.2 fusion.5
  131.8 0.1 copy.88
  131.9 0.4 convolution_multiply_fusion
  132.3 0.4 fusion.2
  132.8 0.2 copy.84
  133.0 0.1 reshape.129
  133.2 0.2 broadcast_in_dim.104
  133.4 0.9 bitcast_multiply_fusion
  134.4 0.1 fusion.27
  134.6 74.9 %psum.15 = f32[64,12]{1,0:T(8,128)S(1)} all-reduce(f32[64,12]{1,0:T(8,128)S(1)} %get-tuple-element.10), channel_id=1, replica_groups=mesh['group'=32,'tp'=8] {'group','tp'}, use_global_device_ids=true, to_apply=%region_7.8 | all-reduce | flops 768 | bytes 6144 | tf_op jit(solution)/shard_map/psum | solution.py:60
  209.7 168.6 %all-reduce.2.cloned.1.call-done = f32[64,1536]{1,0:T(8,128)} async-done(((f32[64,1536]{1,0:T(8,128)}), f32[64,1536]{1,0:T(8,128)}) %all-reduce.2.cloned.1.call-update) | async-done | bytes 393232 | tf_op jit(solution)/shard_map/psum | solution.py:60
  378.3 2.7 convolution_bitcast_fusion
  381.0 39.5 %reduce-scatter.4.cloned.1.call-done = f32[384,2]{1,0:T(8,128)} async-done(((f32[3072,2]{1,0:T(8,128)}), f32[384,2]{1,0:T(8,128)}) %reduce-scatter.4.cloned.1.call-update) | async-done | bytes 3088
  420.5 1.6 copy.95
  (35 shorter events, 0.7 us)
Async XLA Ops:
  6.5 1.4 copy-start
  6.5 46.4 %copy-start.1 = (s32[64]{0:T(128)S(1)}, s32[64]{0:T(128)}, u32[]{:S(2)}) copy-start(s32[64]{0:T(128)} %param.11) | copy-start | bytes 772
  6.5 371.7 %all-reduce.2.cloned.1.call-start = ((), (), s32[]{:S(2)}) async-start(), calls=%async_computation.1 | async-start | bytes 786432 | tf_op jit(solution)/shard_map/psum | solution.py:60
  133.1 245.2 %copy-start.2 = (bf16[192,3072]{1,0:T(8,128)(2,1)S(1)}, bf16[192,3072]{1,0:T(8,128)(2,1)}, u32[]{:S(2)}) copy-start(bf16[192,3072]{1,0:T(8,128)(2,1)} %param.8) | copy-start | bytes 3538948
  134.3 286.2 %reduce-scatter.4.cloned.1.call-start = ((), (), s32[]{:S(2)}) async-start(), calls=%async_computation.2 | async-start | bytes 1769472
Sparse Core Ops, SparseCore 0:
  134.4 243.8 all-reduce.1
  381.1 39.3 reduce-scatter.3
where the time goes:
time: 430 us; the launch traced here: 429 us
  waiting for transfers between devices  208 us (48%)
  blocking collectives  193 us (45%)
  between operations  13.6 us (3%)
  local copies, waits for them, and re-layouts  6.81 us (2%)
  matrix products  5.21 us (1%)
    psum x1, waiting for transfers between devices, on_device(): lax.psum((req_total * rescale, req_sums * jnp.repeat(rescale, HEAD_DIM, a...  169 us
    psum x1, blocking collectives, on_device(): lax.psum((req_total * rescale, req_sums * jnp.repeat(rescale, HEAD_DIM, a...  74.9 us
    pmax x1, blocking collectives, on_device(): peak_all = lax.pmax(req_top, ('group', 'tp'))  74 us
    unnamed x3, waiting for transfers between devices  39.6 us
    all_gather x1, blocking collectives, on_device(): queries = lax.all_gather(qkv[:, :qdim], 'group', axis=0, tiled=True)  24.7 us
    all_gather x1, blocking collectives, on_device(): qkv = lax.all_gather(columns, 'tp', axis=1, tiled=True)  19.1 us
  transfers between devices with their start and end apart: 2, of which 2 were waited for; matrix products, arithmetic and copies ran while one was open for 0% of the time, Pallas kernels for 0%

commit v1 on v0

--- a/solution.py
+++ b/solution.py
@@ -58,7 +58,8 @@
     peak_all = lax.pmax(req_top, ("group", "tp"))
     rescale = jnp.exp(req_top - peak_all)
     total_all, sums_all = lax.psum(
-        (req_total * rescale, req_sums * jnp.repeat(rescale, HEAD_DIM, axis=1)), ("group", "tp")
+        lax.psum((req_total * rescale, req_sums * jnp.repeat(rescale, HEAD_DIM, axis=1)), "tp"),
+        "group",
     )
     peak = lax.dynamic_slice_in_dim(peak_all, start, req_grp, 0)
     whole = lax.dynamic_slice_in_dim(total_all, start, req_grp, 0)

time: 430 us -> 445 us (1.035)
  blocking collectives: 193 us -> 253 us
  waiting for transfers between devices: 208 us -> 164 us
    psum x1, waiting for transfers between devices: 169 us -> 0.02 us  [on_device(): lax.psum((req_total * rescale, req_sums * jnp.repeat(rescale, HEAD_DIM, a...]
    psum x0 -> x1, waiting for transfers between devices: none -> 123 us  [on_device(): lax.psum(lax.psum((req_total * rescale, req_sums * jnp.repeat(rescale, HE...]
    psum x0 -> x1, blocking collectives: none -> 106 us  [on_device(): lax.psum(lax.psum((req_total * rescale, req_sums * jnp.repeat(rescale, HE...]
    psum x1, blocking collectives: 74.9 us -> 29 us  [on_device(): lax.psum((req_total * rescale, req_sums * jnp.repeat(rescale, HEAD_DIM, a...]
    unnamed x3 -> x4, waiting for transfers between devices: 39.6 us -> 40.7 us
  transfers between devices with their start and end apart: 2 -> 3, of which waited for: 2 -> 2; matrix products, arithmetic and copies ran while one was open for 0% -> 0% of each run, Pallas kernels for 0% -> 0%
where the time goes in v1:
time: 445 us
  blocking collectives  253 us (57%)
  waiting for transfers between devices  164 us (37%)
  between operations  13.3 us (3%)
  local copies, waits for them, and re-layouts  6.8 us (2%)
  matrix products  5.2 us (1%)
    psum x1, waiting for transfers between devices, on_device(): lax.psum(lax.psum((req_total * rescale, req_sums * jnp.repeat(rescale, HE...  123 us
    psum x1, blocking collectives, on_device(): lax.psum(lax.psum((req_total * rescale, req_sums * jnp.repeat(rescale, HE...  106 us
    pmax x1, blocking collectives, on_device(): peak_all = lax.pmax(req_top, ('group', 'tp'))  74 us
    unnamed x4, waiting for transfers between devices  40.7 us
    psum x1, blocking collectives, on_device(): lax.psum((req_total * rescale, req_sums * jnp.repeat(rescale, HEAD_DIM, a...  29 us
    all_gather x1, blocking collectives, on_device(): queries = lax.all_gather(qkv[:, :qdim], 'group', axis=0, tiled=True)  24.7 us
    all_gather x1, blocking collectives, on_device(): qkv = lax.all_gather(columns, 'tp', axis=1, tiled=True)  19.1 us
  transfers between devices with their start and end apart: 3, of which 2 were waited for; matrix products, arithmetic and copies ran while one was open for 0% of the time, Pallas kernels for 0%

profile of v1, /device:TPU:2, one launch (start us, length us, event | category | flops | bytes accessed | tf_op | source)
XLA Modules:
  0.0 444.8 jit_solution(15075103546881293483)
XLA Ops:
  6.5 1.1 fusion.1
  7.7 0.2 copy-done
  8.0 1.0 convolution_convert_fusion
  9.0 19.1 %all_gather.6 = bf16[2,2048]{1,0:T(2,128)(2,1)S(1)} all-gather(bf16[2,256]{1,0:T(2,128)(2,1)S(1)} %convolution_convert_fusion), channel_id=1, replica_groups=mesh['group'=32,'tp'=8] {'tp'}, dimensions={1}, use_global_device_ids=true | all-gather | bytes 9216 | tf_op jit(solution)/shard_map/all_gather | solution.py:20
  28.1 24.7 %all-gather = bf16[32,2,1536]{2,1,0:T(2,128)(2,1)S(1)} all-gather(bf16[1,2,1536]{2,1,0:T(2,128)(2,1)S(1)} %get-tuple-element.19), channel_id=1, replica_groups=mesh['group'=32,'tp'=8] {'group'}, dimensions={0}, use_global_device_ids=true | all-gather | bytes 202752 | tf_op jit(solution)/shard_map/all_gather | solution.py:21
  52.9 0.6 gather_fusion
  53.5 0.6 gather_fusion.1
  54.1 1.3 fusion.25
  55.4 0.3 copy.96
  55.8 0.3 select_reduce_fusion
  56.1 0.1 copy.81
  56.2 0.1 select_reduce_fusion.1
  56.3 0.1 copy.82
  56.4 0.3 copy.97
  56.7 0.2 convert_reduce_fusion
  56.9 0.1 copy.86
  57.0 74.0 %pmax.7 = f32[64,12]{1,0:T(8,128)S(1)} all-reduce(f32[64,12]{1,0:T(8,128)S(1)} %copy.86), channel_id=1, replica_groups=mesh['group'=32,'tp'=8] {'group','tp'}, use_global_device_ids=true, to_apply=%region_4.5 | all-reduce | flops 768 | bytes 6144 | tf_op jit(solution)/shard_map/pmax | solution.py:58
  131.0 0.6 gather_fusion.2
  131.6 0.2 fusion.5
  131.8 0.1 copy.88
  131.9 0.4 convolution_multiply_fusion
  132.3 0.4 fusion.2
  132.8 0.2 copy.84
  133.2 0.2 broadcast_in_dim.104
  133.3 0.9 bitcast_multiply_fusion
  134.4 0.1 fusion.27
  134.6 29.0 %psum.30 = f32[64,12]{1,0:T(8,128)S(1)} all-reduce(f32[64,12]{1,0:T(8,128)S(1)} %get-tuple-element.10), channel_id=1, replica_groups=mesh['group'=32,'tp'=8] {'tp'}, use_global_device_ids=true, to_apply=%region_8.9 | all-reduce | flops 768 | bytes 6144 | tf_op jit(solution)/shard_map/psum | solution.py:61
  163.6 106.3 %psum.31 = f32[64,12]{1,0:T(8,128)S(1)} all-reduce(f32[64,12]{1,0:T(8,128)S(1)} %psum.30), channel_id=1, replica_groups=mesh['group'=32,'tp'=8] {'group'}, use_global_device_ids=true, to_apply=%region_9.10 | all-reduce | flops 768 | bytes 6144 | tf_op jit(solution)/shard_map/psum | solution.py:60
  270.2 123.1 %all-reduce.5.cloned.1.call-done = f32[64,1536]{1,0:T(8,128)} async-done(((f32[64,1536]{1,0:T(8,128)}), f32[64,1536]{1,0:T(8,128)}) %all-reduce.5.cloned.1.call-update) | async-done | bytes 393232 | tf_op jit(solution)/shard_map/psum | solution.py:60
  393.3 2.7 convolution_bitcast_fusion
  396.0 40.6 %reduce-scatter.4.cloned.1.call-done = f32[384,2]{1,0:T(8,128)} async-done(((f32[3072,2]{1,0:T(8,128)}), f32[384,2]{1,0:T(8,128)}) %reduce-scatter.4.cloned.1.call-update) | async-done | bytes 3088
  436.6 1.6 copy.95
  (39 shorter events, 0.9 us)
Async XLA Ops:
  6.5 1.4 copy-start
  6.5 46.4 %copy-start.1 = (s32[64]{0:T(128)S(1)}, s32[64]{0:T(128)}, u32[]{:S(2)}) copy-start(s32[64]{0:T(128)} %param.11) | copy-start | bytes 772
  6.5 263.5 %all-reduce.3.cloned.1.call-start = ((), (), s32[]{:S(2)}) async-start(), calls=%async_computation.1 | async-start | bytes 786432 | tf_op jit(solution)/shard_map/psum | solution.py:61
  133.1 260.2 %copy-start.2 = (bf16[192,3072]{1,0:T(8,128)(2,1)S(1)}, bf16[192,3072]{1,0:T(8,128)(2,1)}, u32[]{:S(2)}) copy-start(bf16[192,3072]{1,0:T(8,128)(2,1)} %param.8) | copy-start | bytes 3538948
  134.3 259.0 %all-reduce.5.cloned.1.call-start = ((), (), s32[]{:S(2)}) async-start(), calls=%async_computation.2 | async-start | bytes 786432 | tf_op jit(solution)/shard_map/psum | solution.py:60
  270.0 166.6 %reduce-scatter.4.cloned.1.call-start = ((), (), s32[]{:S(2)}) async-start(), calls=%async_computation.3 | async-start | bytes 1769472
Sparse Core Ops, SparseCore 0:
  134.4 69.0 all-reduce.2
  270.2 123.0 all-reduce.4
  396.1 40.4 reduce-scatter.3
